TPU v7x, 512 devices: a whole 4x4x16 slice. The times are simulated.
512 devices in a mesh: space: 64 (over z, x), member: 8 (over y, core).
Axes of the slice: x: 4, y: 4, z: 16, core: 2. Of those that a mesh axis runs over, the one named last changes fastest.
Arguments:
- spectra: float32 [16, 36, 256, 720], P('member', None, 'space'), may hold values from 0.5 to 2
- group_speed: float32 [256, 720], P('space'), may hold values from 0.15 to 0.5
- turning_rate: float32 [256, 720], P('space'), may hold values from -0.28 to 0.28
- obs_cell: int32 [2, 1024], replicated, may hold values from 0 to 184319, as said below
- obs_value: float32 [2, 1024], replicated, may hold values from 0.9 to 1.6
- obs_variance: float32 [2, 1024], replicated, may hold values from 0.001 to 0.01
Outputs:
- analysis: float32 [16, 36, 184320], P(None, None, ('space', 'member'))
Inputs may be any that keep to these rules, and one draw needn't show every extreme that they name: `obs_cell`: every block of 360 consecutive cells starting at a multiple of 360 holds the cell of at least one observation in every batch.
All inputs are finite; a program needn't handle non-finite values.
Results may differ from a plain program's by a relative error of at most 0.0003.
Values sent between devices are 32-bit elements; how exact they have to be, the bound alone decides.
A program may use at most 64 MiB of HBM per device.

v0:
```python
import math
import jax
import jax.numpy as jnp
from jax import lax
from jax.sharding import PartitionSpec as P

LON = 720
STEPS = 4
BATCHES = 2
LOC = 4
HIGH = lax.Precision.HIGHEST


def padded_2(cells, sides, width):
    for axis, dim in sides:
        count = lax.axis_size(axis)
        ends = count - 1
        head = lax.slice_in_dim(cells, 0, width, axis=dim)
        tail = lax.slice_in_dim(cells, cells.shape[dim] - width, cells.shape[dim], axis=dim)
        cells = jnp.concatenate(
            [
                lax.ppermute(tail, axis, [(i, (i + 1) % count) for i in range(ends)]),
                cells,
                lax.ppermute(head, axis, [((i + 1) % count, i) for i in range(ends)]),
            ],
            axis=dim,
        )
    return cells


def copy_for_each(array, axis):
    devices = lax.axis_size(axis)
    return lax.all_to_all(
        jnp.broadcast_to(array[None], (devices, *array.shape)), axis, 0, 0, tiled=True
    )


def over_copies(array, axis):
    everything = copy_for_each(array, axis)
    return jnp.sum(everything, axis=0)


def transport(padded, speed, turning, cosines, sines):
    centre = padded[:, :, 1:-1, :]
    south = padded[:, :, :-2, :]
    north = padded[:, :, 2:, :]
    along_x = speed[None] * cosines[:, None, None]
    along_y = speed[None] * sines[:, None, None]
    along_turn = turning[None] * cosines[:, None, None]
    west = jnp.roll(centre, 1, axis=3)
    east = jnp.roll(centre, -1, axis=3)
    behind = jnp.roll(centre, 1, axis=1)
    ahead = jnp.roll(centre, -1, axis=1)
    result = (
        centre
        - jnp.maximum(along_x, 0.0) * (centre - west)
        - jnp.minimum(along_x, 0.0) * (east - centre)
    )
    result = (
        result
        - jnp.maximum(along_y, 0.0) * (centre - south)
        - jnp.minimum(along_y, 0.0) * (north - centre)
    )
    result = (
        result
        - jnp.maximum(along_turn, 0.0) * (centre - behind)
        - jnp.minimum(along_turn, 0.0) * (ahead - centre)
    )
    return result


def panel(prior, values, variance):
    members = prior.shape[1]
    centre = jnp.mean(prior, axis=1)
    anomaly = prior - centre[:, None]
    spread = jnp.sum(anomaly * anomaly, axis=1) / (members - 1)
    total = spread + variance
    shrink = 1.0 / (1.0 + jnp.sqrt(variance / total))
    weights_obs = ((values - centre)[:, None] - shrink[:, None] * anomaly) / total[:, None]
    outer = anomaly[:, :, None] * weights_obs[:, None, :]
    return outer.reshape(prior.shape[0], members * members) / (members - 1)


def taper(cell_ids, targets):
    lat_gap = cell_ids[:, None] // LON - targets[None, :] // LON
    lon_gap = jnp.abs(cell_ids[:, None] % LON - targets[None, :] % LON)
    lon_gap = jnp.minimum(lon_gap, LON - lon_gap)
    square = (lat_gap * lat_gap + lon_gap * lon_gap).astype(jnp.float32)
    near = jnp.maximum(1.0 - square / (LOC * LOC), 0.0)
    return near * near


def per_device(spectra, group_speed, turning_rate, obs_cell, obs_value, obs_variance):
    local_members, directions, rows, width = spectra.shape
    angles = 2.0 * math.pi * jnp.arange(directions, dtype=jnp.float32) / directions
    cosines = jnp.cos(angles)
    sines = jnp.sin(angles)
    energy = spectra
    for step in range(STEPS):
        padded = padded_2(energy, (("space", 2),), 1)
        energy = transport(padded, group_speed, turning_rate, cosines, sines)
    state = lax.all_to_all(
        energy.reshape(local_members, directions, rows * width),
        "member",
        split_axis=2,
        concat_axis=0,
        tiled=True,
    )
    members, directions, owned = state.shape
    first_cell = (
        lax.axis_index("space") * lax.axis_size("member") + lax.axis_index("member")
    ) * owned
    cell_ids = first_cell + jnp.arange(owned, dtype=jnp.int32)
    for batch in range(BATCHES):
        targets = obs_cell[batch]
        mean_dir = jnp.mean(state, axis=1)
        onehot = (targets[:, None] == cell_ids[None, :]).astype(jnp.float32)
        partial_prior = jnp.dot(onehot, mean_dir.T, precision=HIGH)
        slab_prior = over_copies(partial_prior, "member")
        beside_all = padded_2(slab_prior[None], (("space", 0),), 1)
        prior = jnp.sum(beside_all, axis=0)
        mixing = panel(prior, obs_value[batch], obs_variance[batch])
        gain = jnp.dot(taper(cell_ids, targets), mixing, precision=HIGH).reshape(
            owned, members, members
        )
        deviation = state - jnp.mean(state, axis=0, keepdims=True)
        state = state + jnp.einsum("kdc,ckl->ldc", deviation, gain, precision=HIGH)
    return state


def solution(mesh):
    placed = (P("member", None, "space", None), P("space", None), P("space", None), P(), P(), P())
    return jax.shard_map(
        per_device,
        mesh=mesh,
        in_specs=placed,
        out_specs=P(None, None, ("space", "member")),
        check_vma=False,
    )
```

profile of v0, /device:TPU:230, one launch (start us, length us, event | category | flops | bytes accessed | tf_op | source)
XLA Modules:
  0.0 194.1 jit_solution(2479666879118172591)
XLA Ops:
  1.4 5.0 %collective-permute-start = (f32[2,36,1,720]{3,1,2,0:T(8,128)S(1)}, f32[2,36,1,720]{3,1,2,0:T(8,128)S(1)}, u32[]{:S(2)}, u32[]{:S(2)}) collective-permute-start(f32[2,36,1,720]{3,1,2,0:T(8,128)S(1)} %get-tuple-element.51), channel_id=1, source_target_pairs={{0,8},{8,16},{16,24},{24,32},{32,40},{40,48},{48,56},{56,64},{64,7... | collective-permute-start | bytes 622088 | tf_op jit(solution)/shard_map/ppermute | solution.py:22
  11.5 7.4 %collective-permute-done.1 = f32[2,36,1,720]{3,1,2,0:T(8,128)S(1)} collective-permute-done((f32[2,36,1,720]{3,1,2,0:T(8,128)S(1)}, f32[2,36,1,720]{3,1,2,0:T(8,128)S(1)}, u32[]{:S(2)}, u32[]{:S(2)}) %collective-permute-start.1) | collective-permute-done | bytes 207392 | tf_op jit(solution)/shard_map/ppermute | solution.py:24
  22.5 3.9 %collective-permute-start.3 = (f32[2,36,1,720]{3,1,2,0:T(8,128)S(1)}, f32[2,36,1,720]{3,1,2,0:T(8,128)S(1)}, u32[]{:S(2)}, u32[]{:S(2)}) collective-permute-start(f32[2,36,1,720]{3,1,2,0:T(8,128)S(1)} %get-tuple-element.42), channel_id=1, source_target_pairs={{8,0},{16,8},{24,16},{32,24},{40,32},{48,40},{56,48},{64,56},{72,6... | collective-permute-start | bytes 622088 | tf_op jit(solution)/shard_map/ppermute | solution.py:24
  26.4 2.5 %collective-permute-done.2 = f32[2,36,1,720]{3,1,2,0:T(8,128)S(1)} collective-permute-done((f32[2,36,1,720]{3,1,2,0:T(8,128)S(1)}, f32[2,36,1,720]{3,1,2,0:T(8,128)S(1)}, u32[]{:S(2)}, u32[]{:S(2)}) %collective-permute-start.2) | collective-permute-done | bytes 207392 | tf_op jit(solution)/shard_map/ppermute | solution.py:22
  28.9 5.2 %collective-permute-done.3 = f32[2,36,1,720]{3,1,2,0:T(8,128)S(1)} collective-permute-done((f32[2,36,1,720]{3,1,2,0:T(8,128)S(1)}, f32[2,36,1,720]{3,1,2,0:T(8,128)S(1)}, u32[]{:S(2)}, u32[]{:S(2)}) %collective-permute-start.3) | collective-permute-done | bytes 207392 | tf_op jit(solution)/shard_map/ppermute | solution.py:24
  37.7 3.9 %collective-permute-start.5 = (f32[2,36,1,720]{3,1,2,0:T(8,128)S(1)}, f32[2,36,1,720]{3,1,2,0:T(8,128)S(1)}, u32[]{:S(2)}, u32[]{:S(2)}) collective-permute-start(f32[2,36,1,720]{3,1,2,0:T(8,128)S(1)} %get-tuple-element.32), channel_id=1, source_target_pairs={{8,0},{16,8},{24,16},{32,24},{40,32},{48,40},{56,48},{64,56},{72,6... | collective-permute-start | bytes 622088 | tf_op jit(solution)/shard_map/ppermute | solution.py:24
  41.6 2.2 %collective-permute-done.4 = f32[2,36,1,720]{3,1,2,0:T(8,128)S(1)} collective-permute-done((f32[2,36,1,720]{3,1,2,0:T(8,128)S(1)}, f32[2,36,1,720]{3,1,2,0:T(8,128)S(1)}, u32[]{:S(2)}, u32[]{:S(2)}) %collective-permute-start.4) | collective-permute-done | bytes 207392 | tf_op jit(solution)/shard_map/ppermute | solution.py:22
  43.8 5.2 %collective-permute-done.5 = f32[2,36,1,720]{3,1,2,0:T(8,128)S(1)} collective-permute-done((f32[2,36,1,720]{3,1,2,0:T(8,128)S(1)}, f32[2,36,1,720]{3,1,2,0:T(8,128)S(1)}, u32[]{:S(2)}, u32[]{:S(2)}) %collective-permute-start.5) | collective-permute-done | bytes 207392 | tf_op jit(solution)/shard_map/ppermute | solution.py:24
  52.6 3.9 %collective-permute-start.7 = (f32[2,36,1,720]{3,1,2,0:T(8,128)S(1)}, f32[2,36,1,720]{3,1,2,0:T(8,128)S(1)}, u32[]{:S(2)}, u32[]{:S(2)}) collective-permute-start(f32[2,36,1,720]{3,1,2,0:T(8,128)S(1)} %get-tuple-element.22), channel_id=1, source_target_pairs={{8,0},{16,8},{24,16},{32,24},{40,32},{48,40},{56,48},{64,56},{72,6... | collective-permute-start | bytes 622088 | tf_op jit(solution)/shard_map/ppermute | solution.py:24
  58.7 5.2 %collective-permute-done.7 = f32[2,36,1,720]{3,1,2,0:T(8,128)S(1)} collective-permute-done((f32[2,36,1,720]{3,1,2,0:T(8,128)S(1)}, f32[2,36,1,720]{3,1,2,0:T(8,128)S(1)}, u32[]{:S(2)}, u32[]{:S(2)}) %collective-permute-start.7) | collective-permute-done | bytes 207392 | tf_op jit(solution)/shard_map/ppermute | solution.py:24
  65.9 4.6 %copy.102 = f32[2,36,4,720]{1,0,3,2:T(2,128)S(1)} copy(f32[2,36,4,720]{3,1,2,0:T(8,128)} %fusion.52) | data formatting | bytes 1658880 | tf_op jit(solution)/shard_map/reshape | solution.py:103
  70.5 6.2 %reshape.338 = f32[8,1,25920]{2,1,0:T(1,128)} reshape(f32[2880,2,36]{2,1,0:T(2,128)S(1)} %bitcast.80) | data formatting | bytes 1658880
  76.8 4.6 %all-to-all-start = ((f32[8,1,25920]{2,1,0:T(1,128)}), f32[8,1,25920]{2,1,0:T(1,128)S(1)}, u32[]{:S(2)}, u32[]{:S(2)}) async-start(f32[8,1,25920]{2,1,0:T(1,128)} %reshape.338), calls=%async_computation | async-start | bytes 1662976 | tf_op jit(solution)/shard_map/all_to_all | solution.py:102
  81.5 13.5 %all-to-all-done = f32[8,1,25920]{2,1,0:T(1,128)S(1)} async-done(((f32[8,1,25920]{2,1,0:T(1,128)}), f32[8,1,25920]{2,1,0:T(1,128)S(1)}, u32[]{:S(2)}, u32[]{:S(2)}) %all-to-all-start) | async-done | bytes 829472 | tf_op jit(solution)/shard_map/all_to_all | solution.py:102
  95.6 3.7 %reduce.8 = f32[8,25920]{1,0:T(8,128)} reduce(f32[8,1,25920]{2,1,0:T(1,128)S(1)} %all-to-all-done, f32[]{:T(128)} %broadcast.417), dimensions={1}, to_apply=%all_to_all.19.reduce_sub_computation | reduce | bytes 1658884 | tf_op jit(solution)/shard_map/all_to_all | solution.py:102
  99.4 6.2 %reshape.339 = f32[2880,2,36]{2,1,0:T(2,128)S(1)} reshape(f32[8,25920]{1,0:T(8,128)} %reduce.8) | data formatting | bytes 1658880
  105.5 3.0 %copy.103 = f32[2,36,8,360]{3,2,0,1:T(8,128)} copy(f32[2,36,8,360]{1,0,3,2:T(2,128)S(1)} %bitcast.81) | data formatting | bytes 1658880 | tf_op jit(solution)/shard_map/all_to_all | solution.py:102
  111.7 3.5 %all-to-all-start.1 = ((f32[8,1024,16]{1,2,0:T(8,128)}), f32[8,1024,16]{1,2,0:T(8,128)S(1)}, u32[]{:S(2)}, u32[]{:S(2)}) async-start(f32[8,1024,16]{1,2,0:T(8,128)} %broadcast_in_dim.8), calls=%async_computation.1 | async-start | bytes 1048576 | tf_op jit(solution)/shard_map/all_to_all | solution.py:33
  115.3 10.2 %all-to-all-done.1 = f32[8,1024,16]{1,2,0:T(8,128)S(1)} async-done(((f32[8,1024,16]{1,2,0:T(8,128)}), f32[8,1024,16]{1,2,0:T(8,128)S(1)}, u32[]{:S(2)}, u32[]{:S(2)}) %all-to-all-start.1) | async-done | bytes 524320 | tf_op jit(solution)/shard_map/all_to_all | solution.py:33
  127.5 4.1 %collective-permute-start.9 = (f32[1,1024,16]{1,2,0:T(8,128)S(1)}, f32[1,1024,16]{1,2,0:T(8,128)S(1)}, u32[]{:S(2)}, u32[]{:S(2)}) collective-permute-start(f32[1,1024,16]{1,2,0:T(8,128)S(1)} %bitcast.84), channel_id=1, source_target_pairs={{8,0},{16,8},{24,16},{32,24},{40,32},{48,40},{56,48},{64,56},{72,6... | collective-permute-start | bytes 196616 | tf_op jit(solution)/shard_map/ppermute | solution.py:24
  131.6 2.9 %copy.94 = f32[8,2,36,360]{2,1,0,3:T(2,128)} copy(f32[8,2,36,360]{3,0,1,2:T(8,128)S(1)} %bitcast.82) | data formatting | bytes 1658880 | tf_op jit(solution)/shard_map/all_to_all | solution.py:102
  134.7 2.3 %collective-permute-done.9 = f32[1,1024,16]{1,2,0:T(8,128)S(1)} collective-permute-done((f32[1,1024,16]{1,2,0:T(8,128)S(1)}, f32[1,1024,16]{1,2,0:T(8,128)S(1)}, u32[]{:S(2)}, u32[]{:S(2)}) %collective-permute-start.9) | collective-permute-done | bytes 65568 | tf_op jit(solution)/shard_map/ppermute | solution.py:24
  137.1 2.8 %fusion.20 = f32[360,16,16]{0,2,1:T(8,128)S(1)} fusion(s32[1024]{0:T(1024)S(1)} %bitcast.94, s32[360]{0:T(512)S(1)} %get-tuple-element.84, s32[1024]{0:T(1024)S(1)} %bitcast.95, s32[360]{0:T(512)S(1)} %get-tuple-element.85, f32[1024,16]{0,1:T(8,128)S(1)} %subtract_divide_fusion.1, f32[1024,16]{0,1:T(8,128)S(1)} %get-tuple-element.12), kind=kOutput, calls=%fused_computation.20 | convolution fusion | flops 1137778688 | bytes 510784 | tf_op jit(solution)/shard_map/dot_general | solution.py:123
  142.0 8.5 %fusion.154 = (f32[36,360]{0,1:T(8,128)}, f32[16,360]{0,1:T(8,128)S(1)}, f32[16,36,360]{1,0,2:T(8,128)S(1)}) fusion(f32[16,36,360]{1,0,2:T(8,128)} %bitcast.79, f32[360,16,16]{1,2,0:T(8,128)} %copy.97, f32[36,360]{0,1:T(8,128)S(1)} %copy.96), kind=kOutput, calls=%fused_computation.212 | convolution fusion | flops 40623840 | bytes 2154240 | tf_op jit(solution)/shard_map/kdc,ckl->ldc/dot_general | solution.py:127
  152.3 3.5 %all-to-all-start.2 = ((f32[8,1024,16]{1,2,0:T(8,128)}), f32[8,1024,16]{1,2,0:T(8,128)S(1)}, u32[]{:S(2)}, u32[]{:S(2)}) async-start(f32[8,1024,16]{1,2,0:T(8,128)} %broadcast_in_dim.10), calls=%async_computation.2 | async-start | bytes 1048576 | tf_op jit(solution)/shard_map/all_to_all | solution.py:33
  157.4 8.6 %all-to-all-done.2 = f32[8,1024,16]{1,2,0:T(8,128)S(1)} async-done(((f32[8,1024,16]{1,2,0:T(8,128)}), f32[8,1024,16]{1,2,0:T(8,128)S(1)}, u32[]{:S(2)}, u32[]{:S(2)}) %all-to-all-start.2) | async-done | bytes 524320 | tf_op jit(solution)/shard_map/all_to_all | solution.py:33
  166.1 3.0 %collective-permute-start.10 = (f32[1,1024,16]{1,2,0:T(8,128)S(1)}, f32[1,1024,16]{1,2,0:T(8,128)S(1)}, u32[]{:S(2)}, u32[]{:S(2)}) collective-permute-start(f32[1,1024,16]{1,2,0:T(8,128)S(1)} %bitcast.85), channel_id=1, source_target_pairs={{0,8},{8,16},{16,24},{24,32},{32,40},{40,48},{48,56},{56,64},{64,7... | collective-permute-start | bytes 196616 | tf_op jit(solution)/shard_map/ppermute | solution.py:22
  169.1 3.1 %collective-permute-start.11 = (f32[1,1024,16]{1,2,0:T(8,128)S(1)}, f32[1,1024,16]{1,2,0:T(8,128)S(1)}, u32[]{:S(2)}, u32[]{:S(2)}) collective-permute-start(f32[1,1024,16]{1,2,0:T(8,128)S(1)} %bitcast.86), channel_id=1, source_target_pairs={{8,0},{16,8},{24,16},{32,24},{40,32},{48,40},{56,48},{64,56},{72,6... | collective-permute-start | bytes 196616 | tf_op jit(solution)/shard_map/ppermute | solution.py:24
  173.2 5.4 %collective-permute-done.11 = f32[1,1024,16]{1,2,0:T(8,128)S(1)} collective-permute-done((f32[1,1024,16]{1,2,0:T(8,128)S(1)}, f32[1,1024,16]{1,2,0:T(8,128)S(1)}, u32[]{:S(2)}, u32[]{:S(2)}) %collective-permute-start.11) | collective-permute-done | bytes 65568 | tf_op jit(solution)/shard_map/ppermute | solution.py:24
  178.7 3.5 %fusion.30 = f32[360,16,16]{0,2,1:T(8,128)S(1)} fusion(s32[1024]{0:T(1024)S(1)} %bitcast.91, s32[1024]{0:T(1024)S(1)} %bitcast.92, s32[360]{0:T(512)} %copy-done.6, s32[360]{0:T(512)} %copy-done.7, f32[1024,16]{0,1:T(8,128)S(1)} %subtract_divide_fusion, f32[1024,16]{0,1:T(8,128)S(1)} %get-tuple-element.10), kind=kOutput, calls=%fused_computation.29 | convolution fusion | flops 1137778688 | bytes 510784 | tf_op jit(solution)/shard_map/dot_general | solution.py:123
  184.3 6.7 %bitcast_add_fusion = f32[16,36,360]{1,0,2:T(8,128)} fusion(f32[16,36,360]{1,0,2:T(8,128)S(1)} %get-tuple-element.81, f32[360,16,16]{1,2,0:T(8,128)} %copy.100, f32[36,360]{0,1:T(8,128)S(1)} %copy.99), kind=kOutput, calls=%fused_computation | convolution fusion | flops 40227840 | bytes 2079360 | tf_op jit(solution)/shard_map/kdc,ckl->ldc/dot_general | solution.py:127
  190.9 3.1 %copy.101 = f32[16,36,360]{2,0,1:T(8,128)} copy(f32[16,36,360]{1,0,2:T(8,128)} %bitcast_add_fusion) | data formatting | bytes 1658880 | tf_op jit(solution)/shard_map/add | solution.py:127
  (85 shorter events, 35.9 us)
Async XLA Ops:
  1.4 10.2 %collective-permute-start = (f32[2,36,1,720]{3,1,2,0:T(8,128)S(1)}, f32[2,36,1,720]{3,1,2,0:T(8,128)S(1)}, u32[]{:S(2)}, u32[]{:S(2)}) collective-permute-start(f32[2,36,1,720]{3,1,2,0:T(8,128)S(1)} %get-tuple-element.51), channel_id=1, source_target_pairs={{0,8},{8,16},{16,24},{24,32},{32,40},{40,48},{48,56},{56,64},{64,7... | collective-permute-start | bytes 622088 | tf_op jit(solution)/shard_map/ppermute | solution.py:22
  6.3 12.6 %collective-permute-start.1 = (f32[2,36,1,720]{3,1,2,0:T(8,128)S(1)}, f32[2,36,1,720]{3,1,2,0:T(8,128)S(1)}, u32[]{:S(2)}, u32[]{:S(2)}) collective-permute-start(f32[2,36,1,720]{3,1,2,0:T(8,128)S(1)} %get-tuple-element.52), channel_id=1, source_target_pairs={{8,0},{16,8},{24,16},{32,24},{40,32},{48,40},{56,48},{64,56},{72,6... | collective-permute-start | bytes 622088 | tf_op jit(solution)/shard_map/ppermute | solution.py:24
  8.5 0.7 copy-start.1
  8.5 0.7 copy-start.2
  20.5 8.4 %collective-permute-start.2 = (f32[2,36,1,720]{3,1,2,0:T(8,128)S(1)}, f32[2,36,1,720]{3,1,2,0:T(8,128)S(1)}, u32[]{:S(2)}, u32[]{:S(2)}) collective-permute-start(f32[2,36,1,720]{3,1,2,0:T(8,128)S(1)} %get-tuple-element.41), channel_id=1, source_target_pairs={{0,8},{8,16},{16,24},{24,32},{32,40},{40,48},{48,56},{56,64},{64,7... | collective-permute-start | bytes 622088 | tf_op jit(solution)/shard_map/ppermute | solution.py:22
  22.5 11.7 %collective-permute-start.3 = (f32[2,36,1,720]{3,1,2,0:T(8,128)S(1)}, f32[2,36,1,720]{3,1,2,0:T(8,128)S(1)}, u32[]{:S(2)}, u32[]{:S(2)}) collective-permute-start(f32[2,36,1,720]{3,1,2,0:T(8,128)S(1)} %get-tuple-element.42), channel_id=1, source_target_pairs={{8,0},{16,8},{24,16},{32,24},{40,32},{48,40},{56,48},{64,56},{72,6... | collective-permute-start | bytes 622088 | tf_op jit(solution)/shard_map/ppermute | solution.py:24
  35.7 8.1 %collective-permute-start.4 = (f32[2,36,1,720]{3,1,2,0:T(8,128)S(1)}, f32[2,36,1,720]{3,1,2,0:T(8,128)S(1)}, u32[]{:S(2)}, u32[]{:S(2)}) collective-permute-start(f32[2,36,1,720]{3,1,2,0:T(8,128)S(1)} %get-tuple-element.31), channel_id=1, source_target_pairs={{0,8},{8,16},{16,24},{24,32},{32,40},{40,48},{48,56},{56,64},{64,7... | collective-permute-start | bytes 622088 | tf_op jit(solution)/shard_map/ppermute | solution.py:22
  37.7 11.4 %collective-permute-start.5 = (f32[2,36,1,720]{3,1,2,0:T(8,128)S(1)}, f32[2,36,1,720]{3,1,2,0:T(8,128)S(1)}, u32[]{:S(2)}, u32[]{:S(2)}) collective-permute-start(f32[2,36,1,720]{3,1,2,0:T(8,128)S(1)} %get-tuple-element.32), channel_id=1, source_target_pairs={{8,0},{16,8},{24,16},{32,24},{40,32},{48,40},{56,48},{64,56},{72,6... | collective-permute-start | bytes 622088 | tf_op jit(solution)/shard_map/ppermute | solution.py:24
  50.6 8.1 %collective-permute-start.6 = (f32[2,36,1,720]{3,1,2,0:T(8,128)S(1)}, f32[2,36,1,720]{3,1,2,0:T(8,128)S(1)}, u32[]{:S(2)}, u32[]{:S(2)}) collective-permute-start(f32[2,36,1,720]{3,1,2,0:T(8,128)S(1)} %get-tuple-element.21), channel_id=1, source_target_pairs={{0,8},{8,16},{16,24},{24,32},{32,40},{40,48},{48,56},{56,64},{64,7... | collective-permute-start | bytes 622088 | tf_op jit(solution)/shard_map/ppermute | solution.py:22
  52.6 11.4 %collective-permute-start.7 = (f32[2,36,1,720]{3,1,2,0:T(8,128)S(1)}, f32[2,36,1,720]{3,1,2,0:T(8,128)S(1)}, u32[]{:S(2)}, u32[]{:S(2)}) collective-permute-start(f32[2,36,1,720]{3,1,2,0:T(8,128)S(1)} %get-tuple-element.22), channel_id=1, source_target_pairs={{8,0},{16,8},{24,16},{32,24},{40,32},{48,40},{56,48},{64,56},{72,6... | collective-permute-start | bytes 622088 | tf_op jit(solution)/shard_map/ppermute | solution.py:24
  76.8 4.6 %copy-start.5 = (s32[2,1024]{1,0:T(2,128)S(1)}, s32[2,1024]{1,0:T(2,128)}, u32[]{:S(2)}) copy-start(s32[2,1024]{1,0:T(2,128)} %param.9) | copy-start | bytes 24580
  76.8 18.2 %all-to-all-start = ((f32[8,1,25920]{2,1,0:T(1,128)}), f32[8,1,25920]{2,1,0:T(1,128)S(1)}, u32[]{:S(2)}, u32[]{:S(2)}) async-start(f32[8,1,25920]{2,1,0:T(1,128)} %reshape.338), calls=%async_computation | async-start | bytes 1662976 | tf_op jit(solution)/shard_map/all_to_all | solution.py:102
  108.6 6.7 %copy-start.3 = (f32[2,1024]{1,0:T(2,128)S(1)}, f32[2,1024]{1,0:T(2,128)}, u32[]{:S(2)}) copy-start(f32[2,1024]{1,0:T(2,128)} %param.10) | copy-start | bytes 24580
  108.6 6.7 %copy-start.4 = (f32[2,1024]{1,0:T(2,128)S(1)}, f32[2,1024]{1,0:T(2,128)}, u32[]{:S(2)}) copy-start(f32[2,1024]{1,0:T(2,128)} %param.11) | copy-start | bytes 24580
  110.0 21.7 %copy-start = (f32[2,36,8,360]{3,2,0,1:T(8,128)S(1)}, f32[2,36,8,360]{3,2,0,1:T(8,128)}, u32[]{:S(2)}) copy-start(f32[2,36,8,360]{3,2,0,1:T(8,128)} %copy.103) | copy-start | bytes 2488324
  111.7 13.8 %all-to-all-start.1 = ((f32[8,1024,16]{1,2,0:T(8,128)}), f32[8,1024,16]{1,2,0:T(8,128)S(1)}, u32[]{:S(2)}, u32[]{:S(2)}) async-start(f32[8,1024,16]{1,2,0:T(8,128)} %broadcast_in_dim.8), calls=%async_computation.1 | async-start | bytes 1048576 | tf_op jit(solution)/shard_map/all_to_all | solution.py:33
  115.3 21.8 %copy-start.6 = (s32[360]{0:T(512)}, s32[360]{0:T(512)S(1)}, u32[]{:S(2)}) copy-start(s32[360]{0:T(512)S(1)} %get-tuple-element.84) | copy-start | bytes 4324
  115.3 21.8 %copy-start.7 = (s32[360]{0:T(512)}, s32[360]{0:T(512)S(1)}, u32[]{:S(2)}) copy-start(s32[360]{0:T(512)S(1)} %get-tuple-element.85) | copy-start | bytes 4324
  125.5 9.1 %collective-permute-start.8 = (f32[1,1024,16]{1,2,0:T(8,128)S(1)}, f32[1,1024,16]{1,2,0:T(8,128)S(1)}, u32[]{:S(2)}, u32[]{:S(2)}) collective-permute-start(f32[1,1024,16]{1,2,0:T(8,128)S(1)} %bitcast.83), channel_id=1, source_target_pairs={{0,8},{8,16},{16,24},{24,32},{32,40},{40,48},{48,56},{56,64},{64,7... | collective-permute-start | bytes 196616 | tf_op jit(solution)/shard_map/ppermute | solution.py:22
  127.5 9.5 %collective-permute-start.9 = (f32[1,1024,16]{1,2,0:T(8,128)S(1)}, f32[1,1024,16]{1,2,0:T(8,128)S(1)}, u32[]{:S(2)}, u32[]{:S(2)}) collective-permute-start(f32[1,1024,16]{1,2,0:T(8,128)S(1)} %bitcast.84), channel_id=1, source_target_pairs={{8,0},{16,8},{24,16},{32,24},{40,32},{48,40},{56,48},{64,56},{72,6... | collective-permute-start | bytes 196616 | tf_op jit(solution)/shard_map/ppermute | solution.py:24
  152.3 13.8 %all-to-all-start.2 = ((f32[8,1024,16]{1,2,0:T(8,128)}), f32[8,1024,16]{1,2,0:T(8,128)S(1)}, u32[]{:S(2)}, u32[]{:S(2)}) async-start(f32[8,1024,16]{1,2,0:T(8,128)} %broadcast_in_dim.10), calls=%async_computation.2 | async-start | bytes 1048576 | tf_op jit(solution)/shard_map/all_to_all | solution.py:33
  166.1 7.1 %collective-permute-start.10 = (f32[1,1024,16]{1,2,0:T(8,128)S(1)}, f32[1,1024,16]{1,2,0:T(8,128)S(1)}, u32[]{:S(2)}, u32[]{:S(2)}) collective-permute-start(f32[1,1024,16]{1,2,0:T(8,128)S(1)} %bitcast.85), channel_id=1, source_target_pairs={{0,8},{8,16},{16,24},{24,32},{32,40},{40,48},{48,56},{56,64},{64,7... | collective-permute-start | bytes 196616 | tf_op jit(solution)/shard_map/ppermute | solution.py:22
  169.1 9.5 %collective-permute-start.11 = (f32[1,1024,16]{1,2,0:T(8,128)S(1)}, f32[1,1024,16]{1,2,0:T(8,128)S(1)}, u32[]{:S(2)}, u32[]{:S(2)}) collective-permute-start(f32[1,1024,16]{1,2,0:T(8,128)S(1)} %bitcast.86), channel_id=1, source_target_pairs={{8,0},{16,8},{24,16},{32,24},{40,32},{48,40},{56,48},{64,56},{72,6... | collective-permute-start | bytes 196616 | tf_op jit(solution)/shard_map/ppermute | solution.py:24
where the time goes:
time: 195 us; the launch traced here: 194 us
  waiting for transfers between devices  72 us (37%)
  starting transfers between devices  48.2 us (25%)
  local copies, waits for them, and re-layouts  38.8 us (20%)
  matrix products  23.2 us (12%)
  other arithmetic  11.4 us (6%)
    ppermute x6, waiting for transfers between devices, padded_2(): lax.ppermute(head, axis, [((i + 1) % count, i) for i in range(ends)])  30.8 us
    ppermute x6, starting transfers between devices, padded_2(): lax.ppermute(head, axis, [((i + 1) % count, i) for i in range(ends)])  21 us
    all_to_all x2, waiting for transfers between devices, copy_for_each(): lax.all_to_all(jnp.broadcast_to(array[None], (devices, *array.shape)), ax...  18.8 us
    ppermute x6, starting transfers between devices, padded_2(): lax.ppermute(tail, axis, [(i, (i + 1) % count) for i in range(ends)])  15.6 us
    dot_general x2, matrix products, per_device(): state = state + jnp.einsum('kdc,ckl->ldc', deviation, gain, precision=HIGH)  15.1 us
    unnamed x19, local copies, waits for them, and re-layouts  14.1 us
    all_to_all x1, waiting for transfers between devices, per_device(): lax.all_to_all(energy.reshape(local_members, directions, rows * width), '...  13.5 us
    ppermute x6, waiting for transfers between devices, padded_2(): lax.ppermute(tail, axis, [(i, (i + 1) % count) for i in range(ends)])  8.82 us
  transfers between devices with their start and end apart: 15, of which 13 were waited for; matrix products, arithmetic and copies ran while one was open for 4% of the time, Pallas kernels for 0%

commit v1 on v0

--- a/solution.py
+++ b/solution.py
@@ -99,12 +99,20 @@
     for step in range(STEPS):
         padded = padded_2(energy, (("space", 2),), 1)
         energy = transport(padded, group_speed, turning_rate, cosines, sines)
-    state = lax.all_to_all(
-        energy.reshape(local_members, directions, rows * width),
-        "member",
-        split_axis=2,
-        concat_axis=0,
-        tiled=True,
+    state = jnp.concatenate(
+        lax.all_to_all(
+            jnp.stack(
+                jnp.split(
+                    energy.reshape(local_members, directions, rows * width),
+                    lax.axis_size("member"),
+                    axis=2,
+                )
+            ),
+            "member",
+            0,
+            0,
+        ),
+        axis=0,
     )
     members, directions, owned = state.shape
     first_cell = (

time: 195 us -> 178 us (0.913)
  the two profiles are of different devices: /device:TPU:230 before, /device:TPU:102 now
where the time goes in v1:
time: 178 us; the launch traced here: 177 us
  waiting for transfers between devices  72.5 us (41%)
  starting transfers between devices  47.9 us (27%)
  local copies, waits for them, and re-layouts  26.8 us (15%)
  matrix products  23.2 us (13%)
  other arithmetic  5.75 us (3%)
    ppermute x6, waiting for transfers between devices, padded_2(): lax.ppermute(head, axis, [((i + 1) % count, i) for i in range(ends)])  30.9 us
    ppermute x6, starting transfers between devices, padded_2(): lax.ppermute(head, axis, [((i + 1) % count, i) for i in range(ends)])  20.3 us
    all_to_all x2, waiting for transfers between devices, copy_for_each(): lax.all_to_all(jnp.broadcast_to(array[None], (devices, *array.shape)), ax...  18.8 us
    ppermute x6, starting transfers between devices, padded_2(): lax.ppermute(tail, axis, [(i, (i + 1) % count) for i in range(ends)])  16.2 us
    dot_general x2, matrix products, per_device(): state = state + jnp.einsum('kdc,ckl->ldc', deviation, gain, precision=HIGH)  15.1 us
    all_to_all x1, waiting for transfers between devices, per_device(): lax.all_to_all(jnp.stack(jnp.split(energy.reshape(local_members, directio...  14.1 us
    ppermute x6, waiting for transfers between devices, padded_2(): lax.ppermute(tail, axis, [(i, (i + 1) % count) for i in range(ends)])  8.82 us
    unnamed x22, local copies, waits for them, and re-layouts  7.27 us
  transfers between devices with their start and end apart: 15, of which 13 were waited for; matrix products, arithmetic and copies ran while one was open for 4% of the time, Pallas kernels for 0%

profile of v1, /device:TPU:102, one launch (start us, length us, event | category | flops | bytes accessed | tf_op | source)
XLA Modules:
  0.0 176.7 jit_solution(9308034760938547195)
XLA Ops:
  1.4 5.0 %collective-permute-start = (f32[2,36,1,720]{3,1,2,0:T(8,128)S(1)}, f32[2,36,1,720]{3,1,2,0:T(8,128)S(1)}, u32[]{:S(2)}, u32[]{:S(2)}) collective-permute-start(f32[2,36,1,720]{3,1,2,0:T(8,128)S(1)} %get-tuple-element.51), channel_id=1, source_target_pairs={{0,8},{8,16},{16,24},{24,32},{32,40},{40,48},{48,56},{56,64},{64,7... | collective-permute-start | bytes 622088 | tf_op jit(solution)/shard_map/ppermute | solution.py:22
  6.3 1.9 %collective-permute-start.1 = (f32[2,36,1,720]{3,1,2,0:T(8,128)S(1)}, f32[2,36,1,720]{3,1,2,0:T(8,128)S(1)}, u32[]{:S(2)}, u32[]{:S(2)}) collective-permute-start(f32[2,36,1,720]{3,1,2,0:T(8,128)S(1)} %get-tuple-element.52), channel_id=1, source_target_pairs={{8,0},{16,8},{24,16},{32,24},{40,32},{48,40},{56,48},{64,56},{72,6... | collective-permute-start | bytes 622088 | tf_op jit(solution)/shard_map/ppermute | solution.py:24
  9.6 1.9 %collective-permute-done = f32[2,36,1,720]{3,1,2,0:T(8,128)S(1)} collective-permute-done((f32[2,36,1,720]{3,1,2,0:T(8,128)S(1)}, f32[2,36,1,720]{3,1,2,0:T(8,128)S(1)}, u32[]{:S(2)}, u32[]{:S(2)}) %collective-permute-start) | collective-permute-done | bytes 207392 | tf_op jit(solution)/shard_map/ppermute | solution.py:22
  11.5 7.4 %collective-permute-done.1 = f32[2,36,1,720]{3,1,2,0:T(8,128)S(1)} collective-permute-done((f32[2,36,1,720]{3,1,2,0:T(8,128)S(1)}, f32[2,36,1,720]{3,1,2,0:T(8,128)S(1)}, u32[]{:S(2)}, u32[]{:S(2)}) %collective-permute-start.1) | collective-permute-done | bytes 207392 | tf_op jit(solution)/shard_map/ppermute | solution.py:24
  20.5 1.9 %collective-permute-start.2 = (f32[2,36,1,720]{3,1,2,0:T(8,128)S(1)}, f32[2,36,1,720]{3,1,2,0:T(8,128)S(1)}, u32[]{:S(2)}, u32[]{:S(2)}) collective-permute-start(f32[2,36,1,720]{3,1,2,0:T(8,128)S(1)} %get-tuple-element.41), channel_id=1, source_target_pairs={{0,8},{8,16},{16,24},{24,32},{32,40},{40,48},{48,56},{56,64},{64,7... | collective-permute-start | bytes 622088 | tf_op jit(solution)/shard_map/ppermute | solution.py:22
  22.5 3.9 %collective-permute-start.3 = (f32[2,36,1,720]{3,1,2,0:T(8,128)S(1)}, f32[2,36,1,720]{3,1,2,0:T(8,128)S(1)}, u32[]{:S(2)}, u32[]{:S(2)}) collective-permute-start(f32[2,36,1,720]{3,1,2,0:T(8,128)S(1)} %get-tuple-element.42), channel_id=1, source_target_pairs={{8,0},{16,8},{24,16},{32,24},{40,32},{48,40},{56,48},{64,56},{72,6... | collective-permute-start | bytes 622088 | tf_op jit(solution)/shard_map/ppermute | solution.py:24
  26.4 2.5 %collective-permute-done.2 = f32[2,36,1,720]{3,1,2,0:T(8,128)S(1)} collective-permute-done((f32[2,36,1,720]{3,1,2,0:T(8,128)S(1)}, f32[2,36,1,720]{3,1,2,0:T(8,128)S(1)}, u32[]{:S(2)}, u32[]{:S(2)}) %collective-permute-start.2) | collective-permute-done | bytes 207392 | tf_op jit(solution)/shard_map/ppermute | solution.py:22
  28.9 5.2 %collective-permute-done.3 = f32[2,36,1,720]{3,1,2,0:T(8,128)S(1)} collective-permute-done((f32[2,36,1,720]{3,1,2,0:T(8,128)S(1)}, f32[2,36,1,720]{3,1,2,0:T(8,128)S(1)}, u32[]{:S(2)}, u32[]{:S(2)}) %collective-permute-start.3) | collective-permute-done | bytes 207392 | tf_op jit(solution)/shard_map/ppermute | solution.py:24
  37.7 3.9 %collective-permute-start.5 = (f32[2,36,1,720]{3,1,2,0:T(8,128)S(1)}, f32[2,36,1,720]{3,1,2,0:T(8,128)S(1)}, u32[]{:S(2)}, u32[]{:S(2)}) collective-permute-start(f32[2,36,1,720]{3,1,2,0:T(8,128)S(1)} %get-tuple-element.32), channel_id=1, source_target_pairs={{8,0},{16,8},{24,16},{32,24},{40,32},{48,40},{56,48},{64,56},{72,6... | collective-permute-start | bytes 622088 | tf_op jit(solution)/shard_map/ppermute | solution.py:24
  41.6 2.2 %collective-permute-done.4 = f32[2,36,1,720]{3,1,2,0:T(8,128)S(1)} collective-permute-done((f32[2,36,1,720]{3,1,2,0:T(8,128)S(1)}, f32[2,36,1,720]{3,1,2,0:T(8,128)S(1)}, u32[]{:S(2)}, u32[]{:S(2)}) %collective-permute-start.4) | collective-permute-done | bytes 207392 | tf_op jit(solution)/shard_map/ppermute | solution.py:22
  43.8 5.2 %collective-permute-done.5 = f32[2,36,1,720]{3,1,2,0:T(8,128)S(1)} collective-permute-done((f32[2,36,1,720]{3,1,2,0:T(8,128)S(1)}, f32[2,36,1,720]{3,1,2,0:T(8,128)S(1)}, u32[]{:S(2)}, u32[]{:S(2)}) %collective-permute-start.5) | collective-permute-done | bytes 207392 | tf_op jit(solution)/shard_map/ppermute | solution.py:24
  52.6 3.9 %collective-permute-start.7 = (f32[2,36,1,720]{3,1,2,0:T(8,128)S(1)}, f32[2,36,1,720]{3,1,2,0:T(8,128)S(1)}, u32[]{:S(2)}, u32[]{:S(2)}) collective-permute-start(f32[2,36,1,720]{3,1,2,0:T(8,128)S(1)} %get-tuple-element.22), channel_id=1, source_target_pairs={{8,0},{16,8},{24,16},{32,24},{40,32},{48,40},{56,48},{64,56},{72,6... | collective-permute-start | bytes 622088 | tf_op jit(solution)/shard_map/ppermute | solution.py:24
  56.5 2.2 %collective-permute-done.6 = f32[2,36,1,720]{3,1,2,0:T(8,128)S(1)} collective-permute-done((f32[2,36,1,720]{3,1,2,0:T(8,128)S(1)}, f32[2,36,1,720]{3,1,2,0:T(8,128)S(1)}, u32[]{:S(2)}, u32[]{:S(2)}) %collective-permute-start.6) | collective-permute-done | bytes 207392 | tf_op jit(solution)/shard_map/ppermute | solution.py:22
  58.7 5.2 %collective-permute-done.7 = f32[2,36,1,720]{3,1,2,0:T(8,128)S(1)} collective-permute-done((f32[2,36,1,720]{3,1,2,0:T(8,128)S(1)}, f32[2,36,1,720]{3,1,2,0:T(8,128)S(1)}, u32[]{:S(2)}, u32[]{:S(2)}) %collective-permute-start.7) | collective-permute-done | bytes 207392 | tf_op jit(solution)/shard_map/ppermute | solution.py:24
  72.9 4.5 %all-to-all-start = ((f32[8,2,36,360]{3,1,2,0:T(2,128)}), f32[8,2,36,360]{3,1,2,0:T(2,128)S(1)}, u32[]{:S(2)}, u32[]{:S(2)}) async-start(f32[8,2,36,360]{3,1,2,0:T(2,128)} %fusion.131), calls=%async_computation | async-start | bytes 1769472 | tf_op jit(solution)/shard_map/all_to_all | solution.py:103
  77.4 14.1 %all-to-all-done = f32[8,2,36,360]{3,1,2,0:T(2,128)S(1)} async-done(((f32[8,2,36,360]{3,1,2,0:T(2,128)}), f32[8,2,36,360]{3,1,2,0:T(2,128)S(1)}, u32[]{:S(2)}, u32[]{:S(2)}) %all-to-all-start) | async-done | bytes 829472 | tf_op jit(solution)/shard_map/all_to_all | solution.py:103
  93.8 3.5 %all-to-all-start.1 = ((f32[8,1024,16]{1,2,0:T(8,128)}), f32[8,1024,16]{1,2,0:T(8,128)S(1)}, u32[]{:S(2)}, u32[]{:S(2)}) async-start(f32[8,1024,16]{1,2,0:T(8,128)} %broadcast_in_dim.8), calls=%async_computation.1 | async-start | bytes 1048576 | tf_op jit(solution)/shard_map/all_to_all | solution.py:33
  97.4 10.2 %all-to-all-done.1 = f32[8,1024,16]{1,2,0:T(8,128)S(1)} async-done(((f32[8,1024,16]{1,2,0:T(8,128)}), f32[8,1024,16]{1,2,0:T(8,128)S(1)}, u32[]{:S(2)}, u32[]{:S(2)}) %all-to-all-start.1) | async-done | bytes 524320 | tf_op jit(solution)/shard_map/all_to_all | solution.py:33
  109.5 4.1 %collective-permute-start.9 = (f32[1,1024,16]{1,2,0:T(8,128)S(1)}, f32[1,1024,16]{1,2,0:T(8,128)S(1)}, u32[]{:S(2)}, u32[]{:S(2)}) collective-permute-start(f32[1,1024,16]{1,2,0:T(8,128)S(1)} %bitcast.108), channel_id=1, source_target_pairs={{8,0},{16,8},{24,16},{32,24},{40,32},{48,40},{56,48},{64,56},{72,6... | collective-permute-start | bytes 196616 | tf_op jit(solution)/shard_map/ppermute | solution.py:24
  113.7 3.6 %copy.69 = f32[8,2,36,360]{2,1,0,3:T(2,128)} copy(f32[8,2,36,360]{3,1,2,0:T(2,128)S(1)} %all-to-all-done) | data formatting | bytes 1658880 | tf_op jit(solution)/shard_map/all_to_all | solution.py:103
  119.1 2.8 %fusion.20 = f32[360,16,16]{0,2,1:T(8,128)S(1)} fusion(s32[1024]{0:T(1024)S(1)} %bitcast.118, s32[360]{0:T(512)S(1)} %get-tuple-element.84, s32[1024]{0:T(1024)S(1)} %bitcast.119, s32[360]{0:T(512)S(1)} %get-tuple-element.85, f32[1024,16]{0,1:T(8,128)S(1)} %subtract_divide_fusion.1, f32[1024,16]{0,1:T(8,128)S(1)} %get-tuple-element.12), kind=kOutput, calls=%fused_computation.20 | convolution fusion | flops 1137778688 | bytes 510784 | tf_op jit(solution)/shard_map/dot_general | solution.py:131
  121.9 2.1 %copy.71 = f32[360,16,16]{1,2,0:T(8,128)} copy(f32[360,16,16]{0,2,1:T(8,128)S(1)} %fusion.20) | data formatting | bytes 737280 | tf_op jit(solution)/shard_map/dot_general | solution.py:131
  124.1 8.5 %fusion.162 = (f32[36,360]{0,1:T(8,128)}, f32[16,360]{0,1:T(8,128)S(1)}, f32[16,36,360]{1,0,2:T(8,128)S(1)}) fusion(f32[16,36,360]{1,0,2:T(8,128)} %bitcast.106, f32[360,16,16]{1,2,0:T(8,128)} %copy.71, f32[36,360]{0,1:T(8,128)S(1)} %copy.70), kind=kOutput, calls=%fused_computation.226 | convolution fusion | flops 40623840 | bytes 2154240 | tf_op jit(solution)/shard_map/kdc,ckl->ldc/dot_general | solution.py:135
  134.3 3.5 %all-to-all-start.2 = ((f32[8,1024,16]{1,2,0:T(8,128)}), f32[8,1024,16]{1,2,0:T(8,128)S(1)}, u32[]{:S(2)}, u32[]{:S(2)}) async-start(f32[8,1024,16]{1,2,0:T(8,128)} %broadcast_in_dim.10), calls=%async_computation.2 | async-start | bytes 1048576 | tf_op jit(solution)/shard_map/all_to_all | solution.py:33
  139.5 8.6 %all-to-all-done.2 = f32[8,1024,16]{1,2,0:T(8,128)S(1)} async-done(((f32[8,1024,16]{1,2,0:T(8,128)}), f32[8,1024,16]{1,2,0:T(8,128)S(1)}, u32[]{:S(2)}, u32[]{:S(2)}) %all-to-all-start.2) | async-done | bytes 524320 | tf_op jit(solution)/shard_map/all_to_all | solution.py:33
  148.1 3.6 %collective-permute-start.10 = (f32[1,1024,16]{1,2,0:T(8,128)S(1)}, f32[1,1024,16]{1,2,0:T(8,128)S(1)}, u32[]{:S(2)}, u32[]{:S(2)}) collective-permute-start(f32[1,1024,16]{1,2,0:T(8,128)S(1)} %bitcast.109), channel_id=1, source_target_pairs={{0,8},{8,16},{16,24},{24,32},{32,40},{40,48},{48,56},{56,64},{64,7... | collective-permute-start | bytes 196616 | tf_op jit(solution)/shard_map/ppermute | solution.py:22
  151.7 2.5 %collective-permute-start.11 = (f32[1,1024,16]{1,2,0:T(8,128)S(1)}, f32[1,1024,16]{1,2,0:T(8,128)S(1)}, u32[]{:S(2)}, u32[]{:S(2)}) collective-permute-start(f32[1,1024,16]{1,2,0:T(8,128)S(1)} %bitcast.110), channel_id=1, source_target_pairs={{8,0},{16,8},{24,16},{32,24},{40,32},{48,40},{56,48},{64,56},{72,6... | collective-permute-start | bytes 196616 | tf_op jit(solution)/shard_map/ppermute | solution.py:24
  155.2 6.0 %collective-permute-done.11 = f32[1,1024,16]{1,2,0:T(8,128)S(1)} collective-permute-done((f32[1,1024,16]{1,2,0:T(8,128)S(1)}, f32[1,1024,16]{1,2,0:T(8,128)S(1)}, u32[]{:S(2)}, u32[]{:S(2)}) %collective-permute-start.11) | collective-permute-done | bytes 65568 | tf_op jit(solution)/shard_map/ppermute | solution.py:24
  161.3 3.5 %fusion.30 = f32[360,16,16]{0,2,1:T(8,128)S(1)} fusion(s32[1024]{0:T(1024)S(1)} %bitcast.115, s32[1024]{0:T(1024)S(1)} %bitcast.116, s32[360]{0:T(512)} %copy-done.5, s32[360]{0:T(512)} %copy-done.6, f32[1024,16]{0,1:T(8,128)S(1)} %subtract_divide_fusion, f32[1024,16]{0,1:T(8,128)S(1)} %get-tuple-element.10), kind=kOutput, calls=%fused_computation.29 | convolution fusion | flops 1137778688 | bytes 510784 | tf_op jit(solution)/shard_map/dot_general | solution.py:131
  164.8 2.1 %copy.74 = f32[360,16,16]{1,2,0:T(8,128)} copy(f32[360,16,16]{0,2,1:T(8,128)S(1)} %fusion.30) | data formatting | bytes 737280 | tf_op jit(solution)/shard_map/dot_general | solution.py:131
  166.9 6.7 %bitcast_add_fusion = f32[16,36,360]{1,0,2:T(8,128)} fusion(f32[16,36,360]{1,0,2:T(8,128)S(1)} %get-tuple-element.81, f32[360,16,16]{1,2,0:T(8,128)} %copy.74, f32[36,360]{0,1:T(8,128)S(1)} %copy.73), kind=kOutput, calls=%fused_computation | convolution fusion | flops 40227840 | bytes 2079360 | tf_op jit(solution)/shard_map/kdc,ckl->ldc/dot_general | solution.py:135
  173.6 3.1 %copy.75 = f32[16,36,360]{2,0,1:T(8,128)} copy(f32[16,36,360]{1,0,2:T(8,128)} %bitcast_add_fusion) | data formatting | bytes 1658880 | tf_op jit(solution)/shard_map/add | solution.py:135
  (86 shorter events, 30.7 us)
Async XLA Ops:
  1.4 10.2 %collective-permute-start = (f32[2,36,1,720]{3,1,2,0:T(8,128)S(1)}, f32[2,36,1,720]{3,1,2,0:T(8,128)S(1)}, u32[]{:S(2)}, u32[]{:S(2)}) collective-permute-start(f32[2,36,1,720]{3,1,2,0:T(8,128)S(1)} %get-tuple-element.51), channel_id=1, source_target_pairs={{0,8},{8,16},{16,24},{24,32},{32,40},{40,48},{48,56},{56,64},{64,7... | collective-permute-start | bytes 622088 | tf_op jit(solution)/shard_map/ppermute | solution.py:22
  6.3 12.6 %collective-permute-start.1 = (f32[2,36,1,720]{3,1,2,0:T(8,128)S(1)}, f32[2,36,1,720]{3,1,2,0:T(8,128)S(1)}, u32[]{:S(2)}, u32[]{:S(2)}) collective-permute-start(f32[2,36,1,720]{3,1,2,0:T(8,128)S(1)} %get-tuple-element.52), channel_id=1, source_target_pairs={{8,0},{16,8},{24,16},{32,24},{40,32},{48,40},{56,48},{64,56},{72,6... | collective-permute-start | bytes 622088 | tf_op jit(solution)/shard_map/ppermute | solution.py:24
  8.5 0.7 copy-start
  8.5 0.7 copy-start.1
  20.5 8.4 %collective-permute-start.2 = (f32[2,36,1,720]{3,1,2,0:T(8,128)S(1)}, f32[2,36,1,720]{3,1,2,0:T(8,128)S(1)}, u32[]{:S(2)}, u32[]{:S(2)}) collective-permute-start(f32[2,36,1,720]{3,1,2,0:T(8,128)S(1)} %get-tuple-element.41), channel_id=1, source_target_pairs={{0,8},{8,16},{16,24},{24,32},{32,40},{40,48},{48,56},{56,64},{64,7... | collective-permute-start | bytes 622088 | tf_op jit(solution)/shard_map/ppermute | solution.py:22
  22.5 11.7 %collective-permute-start.3 = (f32[2,36,1,720]{3,1,2,0:T(8,128)S(1)}, f32[2,36,1,720]{3,1,2,0:T(8,128)S(1)}, u32[]{:S(2)}, u32[]{:S(2)}) collective-permute-start(f32[2,36,1,720]{3,1,2,0:T(8,128)S(1)} %get-tuple-element.42), channel_id=1, source_target_pairs={{8,0},{16,8},{24,16},{32,24},{40,32},{48,40},{56,48},{64,56},{72,6... | collective-permute-start | bytes 622088 | tf_op jit(solution)/shard_map/ppermute | solution.py:24
  35.7 8.1 %collective-permute-start.4 = (f32[2,36,1,720]{3,1,2,0:T(8,128)S(1)}, f32[2,36,1,720]{3,1,2,0:T(8,128)S(1)}, u32[]{:S(2)}, u32[]{:S(2)}) collective-permute-start(f32[2,36,1,720]{3,1,2,0:T(8,128)S(1)} %get-tuple-element.31), channel_id=1, source_target_pairs={{0,8},{8,16},{16,24},{24,32},{32,40},{40,48},{48,56},{56,64},{64,7... | collective-permute-start | bytes 622088 | tf_op jit(solution)/shard_map/ppermute | solution.py:22
  37.7 11.4 %collective-permute-start.5 = (f32[2,36,1,720]{3,1,2,0:T(8,128)S(1)}, f32[2,36,1,720]{3,1,2,0:T(8,128)S(1)}, u32[]{:S(2)}, u32[]{:S(2)}) collective-permute-start(f32[2,36,1,720]{3,1,2,0:T(8,128)S(1)} %get-tuple-element.32), channel_id=1, source_target_pairs={{8,0},{16,8},{24,16},{32,24},{40,32},{48,40},{56,48},{64,56},{72,6... | collective-permute-start | bytes 622088 | tf_op jit(solution)/shard_map/ppermute | solution.py:24
  50.6 8.1 %collective-permute-start.6 = (f32[2,36,1,720]{3,1,2,0:T(8,128)S(1)}, f32[2,36,1,720]{3,1,2,0:T(8,128)S(1)}, u32[]{:S(2)}, u32[]{:S(2)}) collective-permute-start(f32[2,36,1,720]{3,1,2,0:T(8,128)S(1)} %get-tuple-element.21), channel_id=1, source_target_pairs={{0,8},{8,16},{16,24},{24,32},{32,40},{40,48},{48,56},{56,64},{64,7... | collective-permute-start | bytes 622088 | tf_op jit(solution)/shard_map/ppermute | solution.py:22
  52.6 11.4 %collective-permute-start.7 = (f32[2,36,1,720]{3,1,2,0:T(8,128)S(1)}, f32[2,36,1,720]{3,1,2,0:T(8,128)S(1)}, u32[]{:S(2)}, u32[]{:S(2)}) collective-permute-start(f32[2,36,1,720]{3,1,2,0:T(8,128)S(1)} %get-tuple-element.22), channel_id=1, source_target_pairs={{8,0},{16,8},{24,16},{32,24},{40,32},{48,40},{56,48},{64,56},{72,6... | collective-permute-start | bytes 622088 | tf_op jit(solution)/shard_map/ppermute | solution.py:24
  68.7 8.6 %copy-start.4 = (s32[2,1024]{1,0:T(2,128)S(1)}, s32[2,1024]{1,0:T(2,128)}, u32[]{:S(2)}) copy-start(s32[2,1024]{1,0:T(2,128)} %param.9) | copy-start | bytes 24580
  72.9 18.7 %all-to-all-start = ((f32[8,2,36,360]{3,1,2,0:T(2,128)}), f32[8,2,36,360]{3,1,2,0:T(2,128)S(1)}, u32[]{:S(2)}, u32[]{:S(2)}) async-start(f32[8,2,36,360]{3,1,2,0:T(2,128)} %fusion.131), calls=%async_computation | async-start | bytes 1769472 | tf_op jit(solution)/shard_map/all_to_all | solution.py:103
  77.4 19.9 %copy-start.2 = (f32[2,1024]{1,0:T(2,128)S(1)}, f32[2,1024]{1,0:T(2,128)}, u32[]{:S(2)}) copy-start(f32[2,1024]{1,0:T(2,128)} %param.10) | copy-start | bytes 24580
  77.4 19.9 %copy-start.3 = (f32[2,1024]{1,0:T(2,128)S(1)}, f32[2,1024]{1,0:T(2,128)}, u32[]{:S(2)}) copy-start(f32[2,1024]{1,0:T(2,128)} %param.11) | copy-start | bytes 24580
  93.8 13.8 %all-to-all-start.1 = ((f32[8,1024,16]{1,2,0:T(8,128)}), f32[8,1024,16]{1,2,0:T(8,128)S(1)}, u32[]{:S(2)}, u32[]{:S(2)}) async-start(f32[8,1024,16]{1,2,0:T(8,128)} %broadcast_in_dim.8), calls=%async_computation.1 | async-start | bytes 1048576 | tf_op jit(solution)/shard_map/all_to_all | solution.py:33
  97.3 21.8 %copy-start.5 = (s32[360]{0:T(512)}, s32[360]{0:T(512)S(1)}, u32[]{:S(2)}) copy-start(s32[360]{0:T(512)S(1)} %get-tuple-element.84) | copy-start | bytes 4324
  97.3 21.8 %copy-start.6 = (s32[360]{0:T(512)}, s32[360]{0:T(512)S(1)}, u32[]{:S(2)}) copy-start(s32[360]{0:T(512)S(1)} %get-tuple-element.85) | copy-start | bytes 4324
  107.6 9.8 %collective-permute-start.8 = (f32[1,1024,16]{1,2,0:T(8,128)S(1)}, f32[1,1024,16]{1,2,0:T(8,128)S(1)}, u32[]{:S(2)}, u32[]{:S(2)}) collective-permute-start(f32[1,1024,16]{1,2,0:T(8,128)S(1)} %bitcast.107), channel_id=1, source_target_pairs={{0,8},{8,16},{16,24},{24,32},{32,40},{40,48},{48,56},{56,64},{64,7... | collective-permute-start | bytes 196616 | tf_op jit(solution)/shard_map/ppermute | solution.py:22
  109.5 9.5 %collective-permute-start.9 = (f32[1,1024,16]{1,2,0:T(8,128)S(1)}, f32[1,1024,16]{1,2,0:T(8,128)S(1)}, u32[]{:S(2)}, u32[]{:S(2)}) collective-permute-start(f32[1,1024,16]{1,2,0:T(8,128)S(1)} %bitcast.108), channel_id=1, source_target_pairs={{8,0},{16,8},{24,16},{32,24},{40,32},{48,40},{56,48},{64,56},{72,6... | collective-permute-start | bytes 196616 | tf_op jit(solution)/shard_map/ppermute | solution.py:24
  134.3 13.8 %all-to-all-start.2 = ((f32[8,1024,16]{1,2,0:T(8,128)}), f32[8,1024,16]{1,2,0:T(8,128)S(1)}, u32[]{:S(2)}, u32[]{:S(2)}) async-start(f32[8,1024,16]{1,2,0:T(8,128)} %broadcast_in_dim.10), calls=%async_computation.2 | async-start | bytes 1048576 | tf_op jit(solution)/shard_map/all_to_all | solution.py:33
  148.1 7.0 %collective-permute-start.10 = (f32[1,1024,16]{1,2,0:T(8,128)S(1)}, f32[1,1024,16]{1,2,0:T(8,128)S(1)}, u32[]{:S(2)}, u32[]{:S(2)}) collective-permute-start(f32[1,1024,16]{1,2,0:T(8,128)S(1)} %bitcast.109), channel_id=1, source_target_pairs={{0,8},{8,16},{16,24},{24,32},{32,40},{40,48},{48,56},{56,64},{64,7... | collective-permute-start | bytes 196616 | tf_op jit(solution)/shard_map/ppermute | solution.py:22
  151.7 9.5 %collective-permute-start.11 = (f32[1,1024,16]{1,2,0:T(8,128)S(1)}, f32[1,1024,16]{1,2,0:T(8,128)S(1)}, u32[]{:S(2)}, u32[]{:S(2)}) collective-permute-start(f32[1,1024,16]{1,2,0:T(8,128)S(1)} %bitcast.110), channel_id=1, source_target_pairs={{8,0},{16,8},{24,16},{32,24},{40,32},{48,40},{56,48},{64,56},{72,6... | collective-permute-start | bytes 196616 | tf_op jit(solution)/shard_map/ppermute | solution.py:24
